TPU v7x, 256 devices: a whole 4x4x8 slice. The times are simulated.
256 devices in a mesh: blk: 32 (over y_lo, z, core), uly: 8 (over y_hi, x).
Axes of the slice: x: 4, y: 4 (y_hi: 2, y_lo: 2; y = y_hi * 2 + y_lo), z: 8, core: 2. Of those that a mesh axis runs over, the one named last changes fastest.
Arguments:
- tokens: bfloat16 [32768, 5120], P(('blk', 'uly')), may hold values from -6 to 6
- query_base: bfloat16 [32768, 5120], P(('blk', 'uly')), may hold values from -9 to 9
- key_base: bfloat16 [32768, 5120], P(('blk', 'uly')), may hold values from -9 to 9
- value_base: bfloat16 [32768, 5120], P(('blk', 'uly')), may hold values from -6 to 6
- out_grad: bfloat16 [32768, 5120], P(('blk', 'uly')), may hold values from -0.059814453 to 0.059814453
- down_q: bfloat16 [5120, 64], replicated, may hold values from -0.078125 to 0.078125
- up_q: bfloat16 [64, 5120], replicated, may hold values from -0.75 to 0.75
- down_v: bfloat16 [5120, 64], replicated, may hold values from -0.078125 to 0.078125
- up_v: bfloat16 [64, 5120], replicated, may hold values from -0.75 to 0.75
Outputs:
- attended: bfloat16 [32768, 5120], P(('blk', 'uly'))
- grad_down_q: bfloat16 [5120, 64], replicated
- grad_up_q: bfloat16 [64, 5120], P(None, 'uly')
- grad_down_v: bfloat16 [5120, 64], replicated
- grad_up_v: bfloat16 [64, 5120], P(None, 'uly')
All inputs are finite; a program needn't handle non-finite values.
Results may differ from a plain program's by a relative error of at most 0.025.
Values may be sent and summed in bfloat16 or wider, within the bound.
No kernel may reach another device: no remote copies, remote signals or barrier semaphores. Data moves between devices by JAX's collectives and lax.ppermute only.
A program may use at most 128 MiB of HBM per device.

v0:
```python
import jax
import jax.numpy as jnp
from jax import lax
from jax.sharding import PartitionSpec as P

HEAD = 128


def passed_along(block, axis, distance):
    devices = range(lax.axis_size(axis))
    route = [(i - distance, i) for i in devices if i - distance in devices]
    return lax.ppermute(block, axis, route)


def inner(left, right):
    return lax.dot_general(
        left, right, (((0,), (0,)), ((), ())), preferred_element_type=jnp.float32
    )


def head_pass(query, keys, values, upstream, usable, scale):
    scores = jnp.dot(query, keys.T, preferred_element_type=jnp.float32) * scale
    scores = jnp.where(usable[None, :], scores, -jnp.inf)
    top = jnp.max(scores, axis=1, keepdims=True)
    total = jnp.sum(jnp.exp(scores - top), axis=1, keepdims=True)
    probs = jnp.exp(scores - top - jnp.log(total)).astype(jnp.bfloat16)
    attended = jnp.dot(probs, values, preferred_element_type=jnp.float32).astype(jnp.bfloat16)
    delta = jnp.sum(
        upstream.astype(jnp.float32) * attended.astype(jnp.float32), axis=1, keepdims=True
    )
    prob_grad = jnp.dot(upstream, values.T, preferred_element_type=jnp.float32)
    score_grad = (probs.astype(jnp.float32) * (prob_grad - delta)).astype(jnp.bfloat16)
    query_grad = (jnp.dot(score_grad, keys, preferred_element_type=jnp.float32) * scale).astype(
        jnp.bfloat16
    )
    value_terms = jnp.dot(probs.T, upstream, preferred_element_type=jnp.float32)
    return (attended, query_grad, value_terms)


def per_device(tokens, query_base, key_base, value_base, out_grad, down_q, up_q, down_v, up_v):
    low_q = jnp.dot(tokens, down_q, preferred_element_type=jnp.float32).astype(jnp.bfloat16)
    low_v = jnp.dot(tokens, down_v, preferred_element_type=jnp.float32).astype(jnp.bfloat16)
    query = (
        query_base.astype(jnp.float32) + jnp.dot(low_q, up_q, preferred_element_type=jnp.float32)
    ).astype(jnp.bfloat16)
    value = (
        value_base.astype(jnp.float32) + jnp.dot(low_v, up_v, preferred_element_type=jnp.float32)
    ).astype(jnp.bfloat16)
    query_h, keys_h, values_h, upstream_h = (
        lax.all_to_all(query, "uly", split_axis=1, concat_axis=0, tiled=True),
        lax.all_to_all(key_base, "uly", split_axis=1, concat_axis=0, tiled=True),
        lax.all_to_all(value, "uly", split_axis=1, concat_axis=0, tiled=True),
        lax.all_to_all(out_grad, "uly", split_axis=1, concat_axis=0, tiled=True),
    )
    rows = query_h.shape[0]
    width = query_h.shape[1]
    heads_here = width // HEAD
    scale = HEAD ** (-0.5)
    earlier = passed_along(jnp.stack([keys_h, values_h]), "blk", 1)
    keys_all = jnp.concatenate([earlier[0], keys_h], 0)
    values_all = jnp.concatenate([earlier[1], values_h], 0)
    column = jnp.arange(2 * rows)
    usable = jnp.logical_or(column >= rows, lax.axis_index("blk") > 0)

    def per_head(index, carry):
        attended, query_grad, own_terms, prior_terms = carry
        start = index * HEAD
        result = head_pass(
            lax.dynamic_slice_in_dim(query_h, start, HEAD, 1),
            lax.dynamic_slice_in_dim(keys_all, start, HEAD, 1),
            lax.dynamic_slice_in_dim(values_all, start, HEAD, 1),
            lax.dynamic_slice_in_dim(upstream_h, start, HEAD, 1),
            usable,
            scale,
        )
        attended = lax.dynamic_update_slice_in_dim(attended, result[0], start, 1)
        query_grad = lax.dynamic_update_slice_in_dim(query_grad, result[1], start, 1)
        prior_terms = lax.dynamic_update_slice_in_dim(prior_terms, result[2][:rows], start, 1)
        own_terms = lax.dynamic_update_slice_in_dim(own_terms, result[2][rows:], start, 1)
        return (attended, query_grad, own_terms, prior_terms)

    empty_half = jnp.zeros((rows, width), jnp.bfloat16)
    empty_full = jnp.zeros((rows, width), jnp.float32)
    attended_h, query_grad_h, own_terms, prior_terms = lax.fori_loop(
        0, heads_here, per_head, (empty_half, empty_half, empty_full, empty_full)
    )
    returned = passed_along(prior_terms, "blk", -1)
    value_grad_h = (own_terms + returned).astype(jnp.bfloat16)
    rank = down_q.shape[1]
    first_col = lax.axis_index("uly") * width
    attended, query_grad, value_grad = (
        lax.all_to_all(attended_h, "uly", split_axis=0, concat_axis=1, tiled=True),
        lax.all_to_all(query_grad_h, "uly", split_axis=0, concat_axis=1, tiled=True),
        lax.all_to_all(value_grad_h, "uly", split_axis=0, concat_axis=1, tiled=True),
    )
    lowrank = jnp.concatenate(
        [
            jnp.dot(query_grad, up_q.T, preferred_element_type=jnp.float32),
            jnp.dot(value_grad, up_v.T, preferred_element_type=jnp.float32),
        ],
        1,
    ).astype(jnp.bfloat16)
    down_terms = inner(tokens, lowrank)
    up_q_terms = inner(low_q, query_grad)
    up_v_terms = inner(low_v, value_grad)
    down_total, up_q_total, up_v_total = lax.psum(
        (down_terms, up_q_terms, up_v_terms), ("blk", "uly")
    )
    up_q_part = lax.dynamic_slice_in_dim(up_q_total, first_col, width, 1)
    up_v_part = lax.dynamic_slice_in_dim(up_v_total, first_col, width, 1)
    return (
        attended,
        down_total[:, :rank].astype(jnp.bfloat16),
        up_q_part.astype(jnp.bfloat16),
        down_total[:, rank:].astype(jnp.bfloat16),
        up_v_part.astype(jnp.bfloat16),
    )


def solution(mesh):
    return jax.shard_map(
        per_device,
        mesh=mesh,
        in_specs=(
            P(("blk", "uly"), None),
            P(("blk", "uly"), None),
            P(("blk", "uly"), None),
            P(("blk", "uly"), None),
            P(("blk", "uly"), None),
            P(),
            P(),
            P(),
            P(),
        ),
        out_specs=(P(("blk", "uly"), None), P(), P(None, "uly"), P(), P(None, "uly")),
        check_vma=False,
    )
```

profile of v0, /device:TPU:7, one launch (start us, length us, event | category | flops | bytes accessed | tf_op | source)
XLA Modules:
  0.0 464.2 jit_solution(9758977872020225476)
XLA Ops:
  6.5 6.8 %all-to-all-start.2 = ((bf16[128,8,640]{2,0,1:T(8,128)(2,1)}), bf16[128,8,640]{2,0,1:T(8,128)(2,1)S(1)}, u32[]{:S(2)}, u32[]{:S(2)}) async-start(bf16[128,8,640]{2,0,1:T(8,128)(2,1)} %bitcast.90), calls=%async_computation.2 | async-start | bytes 2621440 | tf_op jit(solution)/shard_map/all_to_all | solution.py:52
  13.3 2.5 copy.67
  15.8 15.6 %all-to-all-done.2 = bf16[128,8,640]{2,0,1:T(8,128)(2,1)S(1)} async-done(((bf16[128,8,640]{2,0,1:T(8,128)(2,1)}), bf16[128,8,640]{2,0,1:T(8,128)(2,1)S(1)}, u32[]{:S(2)}, u32[]{:S(2)}) %all-to-all-start.2) | async-done | bytes 1310752 | tf_op jit(solution)/shard_map/all_to_all | solution.py:52
  31.4 22.6 %all_to_all.133 = bf16[128,8,640]{2,0,1:T(8,128)(2,1)S(1)} all-to-all(bf16[128,8,640]{2,0,1:T(8,128)(2,1)} %bitcast.91), channel_id=1, replica_groups=mesh['blk'=32,'uly'=8] {'uly'}, dimensions={1} | all-to-all | bytes 2621440 | tf_op jit(solution)/shard_map/all_to_all | solution.py:51
  55.8 5.6 %collective-permute-start = (bf16[2,1024,640]{2,1,0:T(8,128)(2,1)}, bf16[2,1024,640]{2,1,0:T(8,128)(2,1)}, u32[]{:S(2)}, u32[]{:S(2)}) collective-permute-start(bf16[2,1024,640]{2,1,0:T(8,128)(2,1)} %pad_maximum_fusion), channel_id=1, source_target_pairs={{0,8},{8,16},{16,24},{24,32},{32,40},{40,48},{48,56},{56,64},{64,7... | collective-permute-start | bytes 7864328 | tf_op jit(solution)/shard_map/ppermute | solution.py:12
  61.5 2.5 copy.48
  64.0 6.0 %all-to-all-start.3 = ((bf16[128,8,640]{0,2,1:T(8,128)(2,1)}), bf16[128,8,640]{0,2,1:T(8,128)(2,1)}, u32[]{:S(2)}, u32[]{:S(2)}) async-start(bf16[128,8,640]{0,2,1:T(8,128)(2,1)} %bitcast.89), calls=%async_computation.3 | async-start | bytes 2621440 | tf_op jit(solution)/shard_map/all_to_all | solution.py:53
  73.5 34.2 %all-to-all-done.3 = bf16[128,8,640]{0,2,1:T(8,128)(2,1)} async-done(((bf16[128,8,640]{0,2,1:T(8,128)(2,1)}), bf16[128,8,640]{0,2,1:T(8,128)(2,1)}, u32[]{:S(2)}, u32[]{:S(2)}) %all-to-all-start.3) | async-done | bytes 1310752 | tf_op jit(solution)/shard_map/all_to_all | solution.py:53
  107.7 5.8 %all-to-all-start = ((bf16[128,8,640]{2,0,1:T(8,128)(2,1)}), bf16[128,8,640]{2,0,1:T(8,128)(2,1)}, u32[]{:S(2)}, u32[]{:S(2)}) async-start(bf16[128,8,640]{2,0,1:T(8,128)(2,1)} %bitcast.86), calls=%async_computation | async-start | bytes 2621440 | tf_op jit(solution)/shard_map/all_to_all | solution.py:50
  113.5 2.4 copy.49
  118.1 6.8 %pad_maximum_fusion.1 = (bf16[2048,640]{1,0:T(8,128)(2,1)}, bf16[2048,640]{1,0:T(8,128)(2,1)}) fusion(bf16[1024,640]{1,0:T(8,128)(2,1)S(1)} %bitcast.77, bf16[1024,640]{1,0:T(8,128)(2,1)S(1)} %get-tuple-element.289, bf16[1024,640]{1,0:T(8,128)(2,1)S(1)} %bitcast.75, bf16[1024,640]{1,0:T(8,128)(2,1)S(1)} %get-tuple-element.288), kind=kLoop, calls=%fused_computation.33 | loop fusion | flops 10485760 | bytes 10485760 | tf_op jit(solution)/shard_map/concatenate | solution.py:60
  124.8 6.9 %all-to-all-done = bf16[128,8,640]{2,0,1:T(8,128)(2,1)} async-done(((bf16[128,8,640]{2,0,1:T(8,128)(2,1)}), bf16[128,8,640]{2,0,1:T(8,128)(2,1)}, u32[]{:S(2)}, u32[]{:S(2)}) %all-to-all-start) | async-done | bytes 1310752 | tf_op jit(solution)/shard_map/all_to_all | solution.py:50
  136.3 103.0 %while.20 = (s32[]{:T(128)}, bf16[1024,640]{1,0:T(8,128)(2,1)S(1)}, bf16[1024,640]{1,0:T(8,128)(2,1)}, f32[1024,640]{1,0:T(8,128)}, f32[1024,640]{1,0:T(8,128)},...) while((s32[]{:T(128)}, bf16[1024,640]{1,0:T(8,128)(2,1)S(1)}, ...), condition=%wide.region_4.5_spmd.clone, body=%wide.region_0.4_spmd.clone.sunk | while | flops 2718827520 | bytes 67680992 | solution.py:84
  136.3 2.6 fusion.67
  138.9 2.2 exponential_reduce_fusion.2
  141.1 2.3 exponential_convert_fusion.2
  147.2 3.8 multiply_reduce_fusion.2
  151.0 5.6 %fusion.68 = bf16[1024,640]{1,0:T(8,128)(2,1)} fusion(bf16[1024,640]{1,0:T(8,128)(2,1)} %get-tuple-element.383, s32[]{:T(128)S(6)} %select_n.43, bf16[1024,2048]{1,0:T(8,128)(2,1)} %copy-done.1, bf16[1024,128]{1,0:T(8,128)(2,1)S(1)} %constant_dynamic-slice_fusion.2, f32[1024]{0:T(1024)S(1)} %get-tuple-element.364, ...), kind=kOutput, calls=%fused_computation.10.clone.1 | convolution fusion | flops 1082392576 | bytes 5772800 | tf_op jit(solution)/shard_map/while/body/eval_jaxpr/dot_general | solution.py:33
  157.0 2.6 fusion.67
  159.5 2.2 exponential_reduce_fusion.2
  161.8 2.3 exponential_convert_fusion.2
  167.8 3.8 multiply_reduce_fusion.2
  171.6 5.6 %fusion.68 = bf16[1024,640]{1,0:T(8,128)(2,1)} fusion(bf16[1024,640]{1,0:T(8,128)(2,1)} %get-tuple-element.383, s32[]{:T(128)S(6)} %select_n.43, bf16[1024,2048]{1,0:T(8,128)(2,1)} %copy-done.1, bf16[1024,128]{1,0:T(8,128)(2,1)S(1)} %constant_dynamic-slice_fusion.2, f32[1024]{0:T(1024)S(1)} %get-tuple-element.364, ...), kind=kOutput, calls=%fused_computation.10.clone.1 | convolution fusion | flops 1082392576 | bytes 5772800 | tf_op jit(solution)/shard_map/while/body/eval_jaxpr/dot_general | solution.py:33
  177.6 2.6 fusion.67
  180.1 2.2 exponential_reduce_fusion.2
  182.4 2.3 exponential_convert_fusion.2
  188.4 3.8 multiply_reduce_fusion.2
  192.2 5.6 %fusion.68 = bf16[1024,640]{1,0:T(8,128)(2,1)} fusion(bf16[1024,640]{1,0:T(8,128)(2,1)} %get-tuple-element.383, s32[]{:T(128)S(6)} %select_n.43, bf16[1024,2048]{1,0:T(8,128)(2,1)} %copy-done.1, bf16[1024,128]{1,0:T(8,128)(2,1)S(1)} %constant_dynamic-slice_fusion.2, f32[1024]{0:T(1024)S(1)} %get-tuple-element.364, ...), kind=kOutput, calls=%fused_computation.10.clone.1 | convolution fusion | flops 1082392576 | bytes 5772800 | tf_op jit(solution)/shard_map/while/body/eval_jaxpr/dot_general | solution.py:33
  198.2 2.6 fusion.67
  203.0 2.3 exponential_convert_fusion.2
  209.0 3.8 multiply_reduce_fusion.2
  212.8 5.6 %fusion.68 = bf16[1024,640]{1,0:T(8,128)(2,1)} fusion(bf16[1024,640]{1,0:T(8,128)(2,1)} %get-tuple-element.383, s32[]{:T(128)S(6)} %select_n.43, bf16[1024,2048]{1,0:T(8,128)(2,1)} %copy-done.1, bf16[1024,128]{1,0:T(8,128)(2,1)S(1)} %constant_dynamic-slice_fusion.2, f32[1024]{0:T(1024)S(1)} %get-tuple-element.364, ...), kind=kOutput, calls=%fused_computation.10.clone.1 | convolution fusion | flops 1082392576 | bytes 5772800 | tf_op jit(solution)/shard_map/while/body/eval_jaxpr/dot_general | solution.py:33
  218.7 2.6 fusion.67
  221.3 2.2 exponential_reduce_fusion.2
  223.5 2.3 exponential_convert_fusion.2
  229.6 3.8 multiply_reduce_fusion.2
  233.4 5.6 %fusion.68 = bf16[1024,640]{1,0:T(8,128)(2,1)} fusion(bf16[1024,640]{1,0:T(8,128)(2,1)} %get-tuple-element.383, s32[]{:T(128)S(6)} %select_n.43, bf16[1024,2048]{1,0:T(8,128)(2,1)} %copy-done.1, bf16[1024,128]{1,0:T(8,128)(2,1)S(1)} %constant_dynamic-slice_fusion.2, f32[1024]{0:T(1024)S(1)} %get-tuple-element.364, ...), kind=kOutput, calls=%fused_computation.10.clone.1 | convolution fusion | flops 1082392576 | bytes 5772800 | tf_op jit(solution)/shard_map/while/body/eval_jaxpr/dot_general | solution.py:33
  239.3 2.4 collective-permute-start.1
  241.7 24.9 %all_to_all.134 = bf16[8,128,640]{2,1,0:T(8,128)(2,1)} all-to-all(bf16[8,128,640]{2,1,0:T(8,128)(2,1)} %bitcast.88), channel_id=1, replica_groups=mesh['blk'=32,'uly'=8] {'uly'}, dimensions={0} | all-to-all | bytes 2621440 | tf_op jit(solution)/shard_map/all_to_all | solution.py:93
  266.7 5.5 %all-to-all-start.4 = ((bf16[8,128,640]{2,1,0:T(8,128)(2,1)}), bf16[8,128,640]{2,1,0:T(8,128)(2,1)S(1)}, u32[]{:S(2)}, u32[]{:S(2)}) async-start(bf16[8,128,640]{2,1,0:T(8,128)(2,1)} %bitcast.87), calls=%async_computation.4 | async-start | bytes 2621440 | tf_op jit(solution)/shard_map/all_to_all | solution.py:92
  272.6 3.8 add_convert_fusion
  276.4 12.2 %all-to-all-done.4 = bf16[8,128,640]{2,1,0:T(8,128)(2,1)S(1)} async-done(((bf16[8,128,640]{2,1,0:T(8,128)(2,1)}), bf16[8,128,640]{2,1,0:T(8,128)(2,1)S(1)}, u32[]{:S(2)}, u32[]{:S(2)}) %all-to-all-start.4) | async-done | bytes 1310752 | tf_op jit(solution)/shard_map/all_to_all | solution.py:92
  288.7 7.9 %all-to-all-start.6 = ((bf16[8,128,640]{2,1,0:T(8,128)(2,1)}), bf16[8,128,640]{2,1,0:T(8,128)(2,1)}, u32[]{:S(2)}, u32[]{:S(2)}) async-start(bf16[8,128,640]{2,1,0:T(8,128)(2,1)} %bitcast.93), calls=%async_computation.6 | async-start | bytes 2621440 | tf_op jit(solution)/shard_map/all_to_all | solution.py:94
  299.9 2.5 copy.53
  302.4 2.4 copy.56
  305.2 9.5 %all-to-all-done.6 = bf16[8,128,640]{2,1,0:T(8,128)(2,1)} async-done(((bf16[8,128,640]{2,1,0:T(8,128)(2,1)}), bf16[8,128,640]{2,1,0:T(8,128)(2,1)}, u32[]{:S(2)}, u32[]{:S(2)}) %all-to-all-start.6) | async-done | bytes 1310752 | tf_op jit(solution)/shard_map/all_to_all | solution.py:94
  320.5 139.1 %all-reduce.2 = (bf16[5120,128]{0,1:T(8,128)(2,1)}, bf16[64,5120]{1,0:T(8,128)(2,1)S(1)}, bf16[64,5120]{1,0:T(8,128)(2,1)}) all-reduce(f32[5120,128]{0,1:T(8,128)} %convolution_bitcast_fusion, f32[64,5120]{1,0:T(8,128)S(1)} %copy-done.4, f32[64,5120]{1,0:T(8,128)} %fusion.28), channel_id=1, replica_groups=mesh['blk'=32,'uly'=8] {'blk','uly'}, use_global_device_ids=true, to_apply=%region_5.6 | all-reduce | flops 1310720 | bytes 7864320 | tf_op jit(solution)/shard_map/psum | solution.py:106
  459.6 2.4 fusion.25
  (96 shorter events, 52.1 us)
Async XLA Ops:
  0.6 1.3 copy-start
  0.6 3.0 copy-start.10
  6.5 24.9 %all-to-all-start.2 = ((bf16[128,8,640]{2,0,1:T(8,128)(2,1)}), bf16[128,8,640]{2,0,1:T(8,128)(2,1)S(1)}, u32[]{:S(2)}, u32[]{:S(2)}) async-start(bf16[128,8,640]{2,0,1:T(8,128)(2,1)} %bitcast.90), calls=%async_computation.2 | async-start | bytes 2621440 | tf_op jit(solution)/shard_map/all_to_all | solution.py:52
  53.9 1.9 copy-start.2
  55.8 60.1 %collective-permute-start = (bf16[2,1024,640]{2,1,0:T(8,128)(2,1)}, bf16[2,1024,640]{2,1,0:T(8,128)(2,1)}, u32[]{:S(2)}, u32[]{:S(2)}) collective-permute-start(bf16[2,1024,640]{2,1,0:T(8,128)(2,1)} %pad_maximum_fusion), channel_id=1, source_target_pairs={{0,8},{8,16},{16,24},{24,32},{32,40},{40,48},{48,56},{56,64},{64,7... | collective-permute-start | bytes 7864328 | tf_op jit(solution)/shard_map/ppermute | solution.py:12
  64.0 7.8 %copy-start.7 = (bf16[64,5120]{1,0:T(8,128)(2,1)S(1)}, bf16[64,5120]{1,0:T(8,128)(2,1)}, u32[]{:S(2)}) copy-start(bf16[64,5120]{1,0:T(8,128)(2,1)} %param.17) | copy-start | bytes 1966084
  64.0 43.7 %all-to-all-start.3 = ((bf16[128,8,640]{0,2,1:T(8,128)(2,1)}), bf16[128,8,640]{0,2,1:T(8,128)(2,1)}, u32[]{:S(2)}, u32[]{:S(2)}) async-start(bf16[128,8,640]{0,2,1:T(8,128)(2,1)} %bitcast.89), calls=%async_computation.3 | async-start | bytes 2621440 | tf_op jit(solution)/shard_map/all_to_all | solution.py:53
  70.0 1.8 copy-start.11
  107.7 24.0 %all-to-all-start = ((bf16[128,8,640]{2,0,1:T(8,128)(2,1)}), bf16[128,8,640]{2,0,1:T(8,128)(2,1)}, u32[]{:S(2)}, u32[]{:S(2)}) async-start(bf16[128,8,640]{2,0,1:T(8,128)(2,1)} %bitcast.86), calls=%async_computation | async-start | bytes 2621440 | tf_op jit(solution)/shard_map/all_to_all | solution.py:50
  116.0 2.1 copy-start.3
  143.4 2.5 copy-start.1
  164.0 2.5 copy-start.1
  184.6 2.5 copy-start.1
  205.2 2.5 copy-start.1
  225.8 2.5 copy-start.1
  239.3 27.4 %copy-start.6 = (bf16[1024,640]{1,0:T(8,128)(2,1)}, bf16[1024,640]{1,0:T(8,128)(2,1)S(1)}, u32[]{:S(2)}) copy-start(bf16[1024,640]{1,0:T(8,128)(2,1)S(1)} %get-tuple-element.177) | copy-start | bytes 3932164
  239.3 33.3 %collective-permute-start.1 = (f32[1024,640]{1,0:T(8,128)}, f32[1024,640]{1,0:T(8,128)}, u32[]{:S(2)}, u32[]{:S(2)}) collective-permute-start(f32[1024,640]{1,0:T(8,128)} %get-tuple-element.180), channel_id=1, source_target_pairs={{8,0},{16,8},{24,16},{32,24},{40,32},{48,40},{56,48},{64,56},{72,6... | collective-permute-start | bytes 7864328 | tf_op jit(solution)/shard_map/ppermute | solution.py:12
  266.7 22.0 %all-to-all-start.4 = ((bf16[8,128,640]{2,1,0:T(8,128)(2,1)}), bf16[8,128,640]{2,1,0:T(8,128)(2,1)S(1)}, u32[]{:S(2)}, u32[]{:S(2)}) async-start(bf16[8,128,640]{2,1,0:T(8,128)(2,1)} %bitcast.87), calls=%async_computation.4 | async-start | bytes 2621440 | tf_op jit(solution)/shard_map/all_to_all | solution.py:92
  288.7 7.9 %copy-start.5 = (bf16[8,128,640]{2,1,0:T(8,128)(2,1)}, bf16[8,128,640]{2,1,0:T(8,128)(2,1)S(1)}, u32[]{:S(2)}) copy-start(bf16[8,128,640]{2,1,0:T(8,128)(2,1)S(1)} %all-to-all-done.4) | copy-start | bytes 3932164
  288.7 26.1 %all-to-all-start.6 = ((bf16[8,128,640]{2,1,0:T(8,128)(2,1)}), bf16[8,128,640]{2,1,0:T(8,128)(2,1)}, u32[]{:S(2)}, u32[]{:S(2)}) async-start(bf16[8,128,640]{2,1,0:T(8,128)(2,1)} %bitcast.93), calls=%async_computation.6 | async-start | bytes 2621440 | tf_op jit(solution)/shard_map/all_to_all | solution.py:94
  299.9 4.9 %copy-start.8 = (bf16[64,5120]{1,0:T(8,128)(2,1)S(1)}, bf16[64,5120]{1,0:T(8,128)(2,1)}, u32[]{:S(2)}) copy-start(bf16[64,5120]{1,0:T(8,128)(2,1)} %param.17) | copy-start | bytes 1966084
  305.2 11.3 %copy-start.9 = (bf16[64,5120]{1,0:T(8,128)(2,1)S(1)}, bf16[64,5120]{1,0:T(8,128)(2,1)}, u32[]{:S(2)}) copy-start(bf16[64,5120]{1,0:T(8,128)(2,1)} %param.19) | copy-start | bytes 1966084
  318.5 2.0 copy-start.4
where the time goes:
time: 466 us; the launch traced here: 464 us
  blocking collectives  187 us (40%)
  waiting for transfers between devices  78.9 us (17%)
  matrix products  78.2 us (17%)
  local copies, waits for them, and re-layouts  44.3 us (10%)
  starting transfers between devices  40.1 us (9%)
  other arithmetic  34.9 us (7%)
    psum x1, blocking collectives, per_device(): lax.psum((down_terms, up_q_terms, up_v_terms), ('blk', 'uly'))  139 us
    all_to_all x1, waiting for transfers between devices, per_device(): lax.all_to_all(out_grad, 'uly', split_axis=1, concat_axis=0, tiled=True)  34.2 us
    dot_general x5, matrix products, head_pass(): jnp.dot(score_grad, keys, preferred_element_type=jnp.float32) * scale  28.2 us
    all_to_all x1, blocking collectives, per_device(): lax.all_to_all(query_grad_h, 'uly', split_axis=0, concat_axis=1, tiled=True)  24.9 us
    all_to_all x1, blocking collectives, per_device(): lax.all_to_all(key_base, 'uly', split_axis=1, concat_axis=0, tiled=True)  22.6 us
    dot_general x5, matrix products, head_pass(): jnp.dot(probs, values, preferred_element_type=jnp.float32)  19.2 us
    all_to_all x1, waiting for transfers between devices, per_device(): lax.all_to_all(value, 'uly', split_axis=1, concat_axis=0, tiled=True)  15.6 us
    dot_general x5, matrix products, head_pass(): scores = jnp.dot(query, keys.T, preferred_element_type=jnp.float32) * scale  12.8 us
  transfers between devices with their start and end apart: 7, of which 6 were waited for; matrix products, arithmetic and copies ran while one was open for 7% of the time, Pallas kernels for 0%

commit v1 on v0

--- a/solution.py
+++ b/solution.py
@@ -4,6 +4,11 @@
 from jax.sharding import PartitionSpec as P
 
 HEAD = 128
+
+
+def by_each_axis(array, axis_one, axis_two):
+    partial = lax.psum(array, axis_one)
+    return lax.psum(partial, axis_two)
 
 
 def passed_along(block, axis, distance):
@@ -103,8 +108,8 @@
     down_terms = inner(tokens, lowrank)
     up_q_terms = inner(low_q, query_grad)
     up_v_terms = inner(low_v, value_grad)
-    down_total, up_q_total, up_v_total = lax.psum(
-        (down_terms, up_q_terms, up_v_terms), ("blk", "uly")
+    down_total, up_q_total, up_v_total = by_each_axis(
+        (down_terms, up_q_terms, up_v_terms), "uly", "blk"
     )
     up_q_part = lax.dynamic_slice_in_dim(up_q_total, first_col, width, 1)
     up_v_part = lax.dynamic_slice_in_dim(up_v_total, first_col, width, 1)

time: 466 us -> 589 us (1.26)
  waiting for transfers between devices: 78.9 us -> 216 us
  blocking collectives: 187 us -> 151 us
  between operations: 0.8 us -> 14.2 us
    psum x0 -> x1, waiting for transfers between devices: none -> 114 us  [by_each_axis(): partial = lax.psum(array, axis_one)]
    all_to_all x1 -> x0, blocking collectives: 24.9 us -> none  [per_device(): lax.all_to_all(query_grad_h, 'uly', split_axis=0, concat_axis=1, tiled=True)]
    ppermute x2, waiting for transfers between devices: 0.45 us -> 25 us  [passed_along(): return lax.ppermute(block, axis, route)]
    psum x1, blocking collectives: 139 us -> 128 us  [by_each_axis(): return lax.psum(partial, axis_two)]
    all_to_all x0 -> x1, starting transfers between devices: none -> 5.9 us  [per_device(): lax.all_to_all(query_grad_h, 'uly', split_axis=0, concat_axis=1, tiled=True)]
  transfers between devices with their start and end apart: 7 -> 9, of which waited for: 6 -> 7; matrix products, arithmetic and copies ran while one was open for 7% -> 5% of each run, Pallas kernels for 0% -> 0%
where the time goes in v1:
time: 589 us; the launch traced here: 582 us
  waiting for transfers between devices  216 us (37%)
  blocking collectives  151 us (26%)
  matrix products  78.2 us (13%)
  starting transfers between devices  44.5 us (8%)
  local copies, waits for them, and re-layouts  42 us (7%)
  other arithmetic  35 us (6%)
  between operations  14.2 us (2%)
    psum x1, blocking collectives, by_each_axis(): return lax.psum(partial, axis_two)  128 us
    psum x1, waiting for transfers between devices, by_each_axis(): partial = lax.psum(array, axis_one)  114 us
    all_to_all x1, waiting for transfers between devices, per_device(): lax.all_to_all(out_grad, 'uly', split_axis=1, concat_axis=0, tiled=True)  34.2 us
    dot_general x5, matrix products, head_pass(): jnp.dot(score_grad, keys, preferred_element_type=jnp.float32) * scale  28.2 us
    ppermute x2, waiting for transfers between devices, passed_along(): return lax.ppermute(block, axis, route)  25 us
    all_to_all x1, blocking collectives, per_device(): lax.all_to_all(key_base, 'uly', split_axis=1, concat_axis=0, tiled=True)  22.6 us
    dot_general x5, matrix products, head_pass(): jnp.dot(probs, values, preferred_element_type=jnp.float32)  19.2 us
    all_to_all x1, waiting for transfers between devices, per_device(): lax.all_to_all(value, 'uly', split_axis=1, concat_axis=0, tiled=True)  15.6 us
  transfers between devices with their start and end apart: 9, of which 7 were waited for; matrix products, arithmetic and copies ran while one was open for 5% of the time, Pallas kernels for 0%

profile of v1, /device:TPU:7, one launch (start us, length us, event | category | flops | bytes accessed | tf_op | source)
XLA Modules:
  0.0 581.7 jit_solution(11605313608927288274)
XLA Ops:
  13.0 6.8 %all-to-all-start.2 = ((bf16[128,8,640]{2,0,1:T(8,128)(2,1)}), bf16[128,8,640]{2,0,1:T(8,128)(2,1)S(1)}, u32[]{:S(2)}, u32[]{:S(2)}) async-start(bf16[128,8,640]{2,0,1:T(8,128)(2,1)} %bitcast.90), calls=%async_computation.2 | async-start | bytes 2621440 | tf_op jit(solution)/shard_map/all_to_all | solution.py:57
  19.8 2.5 copy.67
  22.3 15.6 %all-to-all-done.2 = bf16[128,8,640]{2,0,1:T(8,128)(2,1)S(1)} async-done(((bf16[128,8,640]{2,0,1:T(8,128)(2,1)}), bf16[128,8,640]{2,0,1:T(8,128)(2,1)S(1)}, u32[]{:S(2)}, u32[]{:S(2)}) %all-to-all-start.2) | async-done | bytes 1310752 | tf_op jit(solution)/shard_map/all_to_all | solution.py:57
  37.9 22.6 %all_to_all.133 = bf16[128,8,640]{2,0,1:T(8,128)(2,1)S(1)} all-to-all(bf16[128,8,640]{2,0,1:T(8,128)(2,1)} %bitcast.91), channel_id=1, replica_groups=mesh['blk'=32,'uly'=8] {'uly'}, dimensions={1} | all-to-all | bytes 2621440 | tf_op jit(solution)/shard_map/all_to_all | solution.py:56
  62.4 5.6 collective-permute-start
  68.0 2.5 copy.48
  70.5 6.0 %all-to-all-start.3 = ((bf16[128,8,640]{0,2,1:T(8,128)(2,1)}), bf16[128,8,640]{0,2,1:T(8,128)(2,1)}, u32[]{:S(2)}, u32[]{:S(2)}) async-start(bf16[128,8,640]{0,2,1:T(8,128)(2,1)} %bitcast.89), calls=%async_computation.3 | async-start | bytes 2621440 | tf_op jit(solution)/shard_map/all_to_all | solution.py:58
  80.0 34.2 %all-to-all-done.3 = bf16[128,8,640]{0,2,1:T(8,128)(2,1)} async-done(((bf16[128,8,640]{0,2,1:T(8,128)(2,1)}), bf16[128,8,640]{0,2,1:T(8,128)(2,1)}, u32[]{:S(2)}, u32[]{:S(2)}) %all-to-all-start.3) | async-done | bytes 1310752 | tf_op jit(solution)/shard_map/all_to_all | solution.py:58
  114.2 5.8 all-to-all-start
  120.0 2.4 copy.49
  124.6 6.7 %pad_maximum_fusion.1 = (bf16[2048,640]{1,0:T(8,128)(2,1)}, bf16[2048,640]{1,0:T(8,128)(2,1)}) fusion(bf16[1024,640]{1,0:T(8,128)(2,1)S(1)} %bitcast.77, bf16[1024,640]{1,0:T(8,128)(2,1)S(1)} %get-tuple-element.292, bf16[1024,640]{1,0:T(8,128)(2,1)S(1)} %bitcast.75, bf16[1024,640]{1,0:T(8,128)(2,1)S(1)} %get-tuple-element.291), kind=kLoop, calls=%fused_computation.33 | loop fusion | flops 10485760 | bytes 10485760 | tf_op jit(solution)/shard_map/concatenate | solution.py:65
  131.3 6.9 %all-to-all-done = bf16[128,8,640]{2,0,1:T(8,128)(2,1)} async-done(((bf16[128,8,640]{2,0,1:T(8,128)(2,1)}), bf16[128,8,640]{2,0,1:T(8,128)(2,1)}, u32[]{:S(2)}, u32[]{:S(2)}) %all-to-all-start) | async-done | bytes 1310752 | tf_op jit(solution)/shard_map/all_to_all | solution.py:55
  142.8 103.0 %while.20 = (s32[]{:T(128)}, bf16[1024,640]{1,0:T(8,128)(2,1)S(1)}, bf16[1024,640]{1,0:T(8,128)(2,1)}, f32[1024,640]{1,0:T(8,128)}, f32[1024,640]{1,0:T(8,128)},...) while((s32[]{:T(128)}, bf16[1024,640]{1,0:T(8,128)(2,1)S(1)}, ...), condition=%wide.region_4.5_spmd.clone, body=%wide.region_0.4_spmd.clone.sunk | while | flops 2718827520 | bytes 67680992 | solution.py:89
  142.8 2.6 fusion.67
  145.4 2.2 exponential_reduce_fusion.2
  147.6 2.3 exponential_convert_fusion.2
  153.7 3.8 multiply_reduce_fusion.2
  157.5 5.6 fusion.68
  163.4 2.6 fusion.67
  166.0 2.2 exponential_reduce_fusion.2
  168.2 2.3 exponential_convert_fusion.2
  174.2 3.8 multiply_reduce_fusion.2
  178.1 5.6 fusion.68
  184.0 2.6 fusion.67
  186.6 2.2 exponential_reduce_fusion.2
  188.8 2.3 exponential_convert_fusion.2
  194.8 3.8 multiply_reduce_fusion.2
  198.6 5.6 fusion.68
  204.6 2.6 fusion.67
  207.1 2.2 exponential_reduce_fusion.2
  209.4 2.3 exponential_convert_fusion.2
  215.5 3.8 multiply_reduce_fusion.2
  219.3 5.6 fusion.68
  225.2 2.6 fusion.67
  230.0 2.3 exponential_convert_fusion.2
  236.1 3.8 multiply_reduce_fusion.2
  239.9 5.6 fusion.68
  245.8 2.4 collective-permute-start.1
  248.2 5.9 %all-to-all-start.5 = ((bf16[8,128,640]{2,1,0:T(8,128)(2,1)}), bf16[8,128,640]{2,1,0:T(8,128)(2,1)S(1)}, u32[]{:S(2)}, u32[]{:S(2)}) async-start(bf16[8,128,640]{2,1,0:T(8,128)(2,1)} %bitcast.88), calls=%async_computation.5 | async-start | bytes 2621440 | tf_op jit(solution)/shard_map/all_to_all | solution.py:98
  254.2 25.0 %collective-permute-done.1 = f32[1024,640]{1,0:T(8,128)} collective-permute-done((f32[1024,640]{1,0:T(8,128)}, f32[1024,640]{1,0:T(8,128)}, u32[]{:S(2)}, u32[]{:S(2)}) %collective-permute-start.1) | collective-permute-done | bytes 2621472 | tf_op jit(solution)/shard_map/ppermute | solution.py:17
  279.1 3.9 add_convert_fusion
  283.0 6.4 %all-to-all-start.6 = ((bf16[8,128,640]{2,1,0:T(8,128)(2,1)}), bf16[8,128,640]{2,1,0:T(8,128)(2,1)}, u32[]{:S(2)}, u32[]{:S(2)}) async-start(bf16[8,128,640]{2,1,0:T(8,128)(2,1)} %bitcast.93), calls=%async_computation.6 | async-start | bytes 2621440 | tf_op jit(solution)/shard_map/all_to_all | solution.py:99
  293.2 7.5 %all-to-all-done.6 = bf16[8,128,640]{2,1,0:T(8,128)(2,1)} async-done(((bf16[8,128,640]{2,1,0:T(8,128)(2,1)}), bf16[8,128,640]{2,1,0:T(8,128)(2,1)}, u32[]{:S(2)}, u32[]{:S(2)}) %all-to-all-start.6) | async-done | bytes 1310752 | tf_op jit(solution)/shard_map/all_to_all | solution.py:99
  306.6 5.6 all-to-all-start.4
  312.1 13.3 %all-to-all-done.4 = bf16[8,128,640]{2,1,0:T(8,128)(2,1)S(1)} async-done(((bf16[8,128,640]{2,1,0:T(8,128)(2,1)}), bf16[8,128,640]{2,1,0:T(8,128)(2,1)S(1)}, u32[]{:S(2)}, u32[]{:S(2)}) %all-to-all-start.4) | async-done | bytes 1310752 | tf_op jit(solution)/shard_map/all_to_all | solution.py:97
  326.9 2.4 copy.56
  329.3 113.7 %all-reduce.5.cloned.1.call-done = (f32[5120,128]{0,1:T(8,128)}, f32[64,5120]{1,0:T(8,128)}, f32[64,5120]{1,0:T(8,128)}) async-done(((f32[5120,128]{0,1:T(8,128)}, f32[64,5120]{1,0:T(8,128)}, f32[64,5120]{1,0:T(8,128)}), (f32[5120,128]{0,1:T(8,128)}, f32[64,5120]{1,0:T(8,128)}, f32[64,5120]{1,0:T(8,128)})) %all-reduce.5.cloned.1.call-update) | async-done | bytes 5242896 | tf_op jit(solution)/shard_map/psum | solution.py:10
  443.0 128.5 %all-reduce.6 = (bf16[5120,128]{0,1:T(8,128)(2,1)S(1)}, bf16[64,5120]{1,0:T(8,128)(2,1)S(1)}, bf16[64,5120]{1,0:T(8,128)(2,1)}) all-reduce(f32[5120,128]{0,1:T(8,128)} %get-tuple-element.282, f32[64,5120]{1,0:T(8,128)} %get-tuple-element.283, f32[64,5120]{1,0:T(8,128)} %get-tuple-element.284), channel_id=1, replica_groups=mesh['blk'=32,'uly'=8] {'blk'}, use_global_device_ids=true, to_apply=%region_6.7 | all-reduce | flops 1310720 | bytes 7864320 | tf_op jit(solution)/shard_map/psum | solution.py:11
  (98 shorter events, 54.3 us)
Async XLA Ops:
  7.2 1.3 copy-start
  7.2 3.0 copy-start.9
  13.0 24.9 %all-to-all-start.2 = ((bf16[128,8,640]{2,0,1:T(8,128)(2,1)}), bf16[128,8,640]{2,0,1:T(8,128)(2,1)S(1)}, u32[]{:S(2)}, u32[]{:S(2)}) async-start(bf16[128,8,640]{2,0,1:T(8,128)(2,1)} %bitcast.90), calls=%async_computation.2 | async-start | bytes 2621440 | tf_op jit(solution)/shard_map/all_to_all | solution.py:57
  60.5 1.9 copy-start.2
  62.4 60.1 %collective-permute-start = (bf16[2,1024,640]{2,1,0:T(8,128)(2,1)}, bf16[2,1024,640]{2,1,0:T(8,128)(2,1)}, u32[]{:S(2)}, u32[]{:S(2)}) collective-permute-start(bf16[2,1024,640]{2,1,0:T(8,128)(2,1)} %pad_maximum_fusion), channel_id=1, source_target_pairs={{0,8},{8,16},{16,24},{24,32},{32,40},{40,48},{48,56},{56,64},{64,7... | collective-permute-start | bytes 7864328 | tf_op jit(solution)/shard_map/ppermute | solution.py:17
  70.5 7.8 %copy-start.6 = (bf16[64,5120]{1,0:T(8,128)(2,1)S(1)}, bf16[64,5120]{1,0:T(8,128)(2,1)}, u32[]{:S(2)}) copy-start(bf16[64,5120]{1,0:T(8,128)(2,1)} %param.17) | copy-start | bytes 1966084
  70.5 43.7 %all-to-all-start.3 = ((bf16[128,8,640]{0,2,1:T(8,128)(2,1)}), bf16[128,8,640]{0,2,1:T(8,128)(2,1)}, u32[]{:S(2)}, u32[]{:S(2)}) async-start(bf16[128,8,640]{0,2,1:T(8,128)(2,1)} %bitcast.89), calls=%async_computation.3 | async-start | bytes 2621440 | tf_op jit(solution)/shard_map/all_to_all | solution.py:58
  76.5 1.8 copy-start.10
  114.2 24.0 %all-to-all-start = ((bf16[128,8,640]{2,0,1:T(8,128)(2,1)}), bf16[128,8,640]{2,0,1:T(8,128)(2,1)}, u32[]{:S(2)}, u32[]{:S(2)}) async-start(bf16[128,8,640]{2,0,1:T(8,128)(2,1)} %bitcast.85), calls=%async_computation | async-start | bytes 2621440 | tf_op jit(solution)/shard_map/all_to_all | solution.py:55
  122.5 2.1 copy-start.3
  149.9 2.5 copy-start.1
  170.5 2.5 copy-start.1
  191.1 2.5 copy-start.1
  211.6 2.5 copy-start.1
  232.3 2.5 copy-start.1
  245.8 2.4 copy-start.5
  245.8 33.3 %collective-permute-start.1 = (f32[1024,640]{1,0:T(8,128)}, f32[1024,640]{1,0:T(8,128)}, u32[]{:S(2)}, u32[]{:S(2)}) collective-permute-start(f32[1024,640]{1,0:T(8,128)} %get-tuple-element.180), channel_id=1, source_target_pairs={{8,0},{16,8},{24,16},{32,24},{40,32},{48,40},{56,48},{64,56},{72,6... | collective-permute-start | bytes 7864328 | tf_op jit(solution)/shard_map/ppermute | solution.py:17
  248.2 34.8 %all-to-all-start.5 = ((bf16[8,128,640]{2,1,0:T(8,128)(2,1)}), bf16[8,128,640]{2,1,0:T(8,128)(2,1)S(1)}, u32[]{:S(2)}, u32[]{:S(2)}) async-start(bf16[8,128,640]{2,1,0:T(8,128)(2,1)} %bitcast.88), calls=%async_computation.5 | async-start | bytes 2621440 | tf_op jit(solution)/shard_map/all_to_all | solution.py:98
  283.0 6.4 %copy-start.4 = (bf16[8,128,640]{2,1,0:T(8,128)(2,1)}, bf16[8,128,640]{2,1,0:T(8,128)(2,1)S(1)}, u32[]{:S(2)}) copy-start(bf16[8,128,640]{2,1,0:T(8,128)(2,1)S(1)} %all-to-all-done.5) | copy-start | bytes 3932164
  283.0 8.2 %copy-start.7 = (bf16[64,5120]{1,0:T(8,128)(2,1)S(1)}, bf16[64,5120]{1,0:T(8,128)(2,1)}, u32[]{:S(2)}) copy-start(bf16[64,5120]{1,0:T(8,128)(2,1)} %param.17) | copy-start | bytes 1966084
  283.0 17.7 %all-to-all-start.6 = ((bf16[8,128,640]{2,1,0:T(8,128)(2,1)}), bf16[8,128,640]{2,1,0:T(8,128)(2,1)}, u32[]{:S(2)}, u32[]{:S(2)}) async-start(bf16[8,128,640]{2,1,0:T(8,128)(2,1)} %bitcast.93), calls=%async_computation.6 | async-start | bytes 2621440 | tf_op jit(solution)/shard_map/all_to_all | solution.py:99
  289.4 153.6 %all-reduce.5.cloned.1.call-start = ((), (), s32[]{:S(2)}) async-start(), calls=%async_computation.7 | async-start | bytes 10485760 | tf_op jit(solution)/shard_map/psum | solution.py:10
  291.6 11.0 %copy-start.8 = (bf16[64,5120]{1,0:T(8,128)(2,1)S(1)}, bf16[64,5120]{1,0:T(8,128)(2,1)}, u32[]{:S(2)}) copy-start(bf16[64,5120]{1,0:T(8,128)(2,1)} %param.19) | copy-start | bytes 1966084
  306.6 18.8 %all-to-all-start.4 = ((bf16[8,128,640]{2,1,0:T(8,128)(2,1)}), bf16[8,128,640]{2,1,0:T(8,128)(2,1)S(1)}, u32[]{:S(2)}, u32[]{:S(2)}) async-start(bf16[8,128,640]{2,1,0:T(8,128)(2,1)} %bitcast.87), calls=%async_computation.4 | async-start | bytes 2621440 | tf_op jit(solution)/shard_map/all_to_all | solution.py:97
Sparse Core Ops, SparseCore 0:
  306.7 136.2 all-reduce.4
